TPU v7x, 32 devices: a whole 2x2x4 slice. The times are simulated.
32 devices in a mesh: groups: 2 (over y), pool: 4 (over x, core), tp: 4 (over z).
Axes of the slice: x: 2, y: 2, z: 4, core: 2. Of those that a mesh axis runs over, the one named last changes fastest.
Arguments:
- queries: bfloat16 [192, 16384], P(('groups', 'pool', 'tp')), parts along dimension 0, may hold values from -6 to 6
- cached_entries: bfloat16 [192, 512, 512], P(('groups', 'pool', 'tp')), parts along dimension 0, may hold values from -4.5 to 4.5
- new_entry: bfloat16 [192, 512], P(('groups', 'pool', 'tp')), parts along dimension 0, may hold values from -4.5 to 4.5
- lengths: int32 [192], P(('groups', 'pool', 'tp')), parts along dimension 0, may hold values from 2 to 512, as said below
- residual: bfloat16 [192, 7168], P(('groups', 'pool'), 'tp'), parts along dimension 0, may hold values from -40 to 40
- out_weight: bfloat16 [16384, 7168], P('pool', 'tp'), may hold values from -0.046875 to 0.046875
- norm_gain: bfloat16 [7168], P('tp'), may hold values from 0.5 to 1.5
- gate_weight: bfloat16 [7168, 18432], P('tp', 'pool'), may hold values from -0.0625 to 0.0625
- up_weight: bfloat16 [7168, 18432], P('tp', 'pool'), may hold values from -0.0625 to 0.0625
- down_weight: bfloat16 [18432, 7168], P('pool', 'tp'), may hold values from -0.046875 to 0.046875
Outputs:
- layer_out: bfloat16 [192, 7168], P(('groups', 'pool'), 'tp'), parts along dimension 0
There are 2 independent parts, one for each index of `groups`. A program takes and returns all parts, laid end to end along the dimension named above; an argument that names none is the same for every part. Nothing has to cross between parts.
Inputs may be any that keep to these rules, and one draw needn't show every extreme that they name: `lengths`: every request has at least 2 positions in use and at most 512; some request of every draw has exactly 512.
All inputs are finite; a program needn't handle non-finite values.
Results may differ from a plain program's by a relative error of at most 0.009.
Values may be sent and summed in bfloat16 or wider, within the bound.
A program may use at most 192 MiB of HBM per device.

v0:
```python
import math

import jax
import jax.numpy as jnp
from jax import lax
from jax.sharding import PartitionSpec as P

D = 7168
HEADS = 64
HD = 256


epsilon = 1e-06


def attend(queries, cached_entries, new_entry, lengths):
    amount = queries.shape[0]
    query_heads = queries.reshape(amount, HEADS, HD)
    key_rows = cached_entries[:, :, :HD]
    value_rows = cached_entries[:, :, HD:]
    factor = 1.0 / math.sqrt(HD)
    scores = (
        jnp.einsum("rhd,rld->rhl", query_heads, key_rows, preferred_element_type=jnp.float32)
        * factor
    )
    own_score = (
        jnp.einsum("rhd,rd->rh", query_heads, new_entry[:, :HD], preferred_element_type=jnp.float32)
        * factor
    )
    positions = lax.broadcasted_iota(jnp.int32, scores.shape, 2)
    usable = positions < lengths[:, None, None]
    scores = jnp.where(usable, scores, -jnp.inf)
    peak_score = jnp.maximum(jnp.max(scores, axis=2), own_score)
    weights_raw = jnp.where(usable, jnp.exp(scores - peak_score[:, :, None]), 0.0)
    own_raw = jnp.exp(own_score - peak_score)
    totals = jnp.sum(weights_raw, axis=2) + own_raw
    weights = (weights_raw / totals[:, :, None]).astype(jnp.bfloat16)
    own_weight = (own_raw / totals).astype(jnp.bfloat16)
    mixture = jnp.einsum("rhl,rld->rhd", weights, value_rows, preferred_element_type=jnp.float32)
    mixture = mixture + own_weight.astype(jnp.float32)[:, :, None] * new_entry[:, None, HD:].astype(
        jnp.float32
    )
    return mixture.reshape(amount, HEADS * HD).astype(jnp.bfloat16)


def finish_rows(
    queries,
    cached_entries,
    new_entry,
    lengths,
    resid_rows,
    out_weight,
    norm_gain,
    gate_weight,
    up_weight,
    down_weight,
):
    shard_count = lax.axis_size("tp")
    pool_at = lax.axis_index("pool")
    attended = attend(queries, cached_entries, new_entry, lengths)
    columns = lax.all_gather(attended, "tp", axis=0, tiled=True)
    spread = lax.all_to_all(columns, "pool", split_axis=1, concat_axis=0, tiled=True)
    block_rows = shard_count * queries.shape[0]
    resid_flat = resid_rows.reshape(block_rows, resid_rows.shape[2]).astype(jnp.float32)
    gain_row = norm_gain.astype(jnp.float32)[None, :]
    partial_value = jnp.dot(spread, out_weight, preferred_element_type=jnp.float32)
    own_rows = (
        lax.dynamic_slice_in_dim(partial_value, pool_at * block_rows, block_rows, 0) + resid_flat
    )
    summand = lax.dynamic_update_slice_in_dim(partial_value, own_rows, pool_at * block_rows, 0)
    post_attn = lax.psum(summand, "pool")
    scaled = (post_attn * gain_row).astype(jnp.bfloat16)
    squares = jnp.sum(post_attn * post_attn, axis=1)
    own_post = lax.dynamic_slice_in_dim(post_attn, pool_at * block_rows, block_rows, 0)
    gate_part = jnp.dot(scaled, gate_weight, preferred_element_type=jnp.float32)
    up_part = jnp.dot(scaled, up_weight, preferred_element_type=jnp.float32)
    gate_sum, up_sum, square_sum = (
        lax.psum(gate_part.astype(jnp.bfloat16), "tp").astype(jnp.float32),
        lax.psum(up_part.astype(jnp.bfloat16), "tp").astype(jnp.float32),
        lax.psum(squares.astype(jnp.bfloat16), "tp").astype(jnp.float32),
    )
    inv_rms = lax.rsqrt(square_sum / D + epsilon)
    hidden = (jax.nn.silu(gate_sum * inv_rms[:, None]) * (up_sum * inv_rms[:, None])).astype(
        jnp.bfloat16
    )
    down_sum = lax.psum_scatter(
        jnp.dot(hidden, down_weight, preferred_element_type=jnp.float32).astype(jnp.bfloat16),
        "pool",
        scatter_dimension=0,
        tiled=True,
    ).astype(jnp.float32)
    return (own_post + down_sum).astype(jnp.bfloat16)


def on_device(
    queries,
    cached_entries,
    new_entry,
    lengths,
    residual,
    out_weight,
    norm_gain,
    gate_weight,
    up_weight,
    down_weight,
):
    shard_count = lax.axis_size("tp")
    amount = queries.shape[0]
    resid_rows = residual.reshape(shard_count, amount, residual.shape[1])
    result = finish_rows(
        queries,
        cached_entries,
        new_entry,
        lengths,
        resid_rows,
        out_weight,
        norm_gain,
        gate_weight,
        up_weight,
        down_weight,
    )
    return result


def solution(mesh):
    placed = (
        P(("groups", "pool", "tp"), None),
        P(("groups", "pool", "tp"), None, None),
        P(("groups", "pool", "tp"), None),
        P(("groups", "pool", "tp")),
        P(("groups", "pool"), "tp"),
        P("pool", "tp"),
        P("tp"),
        P("tp", "pool"),
        P("tp", "pool"),
        P("pool", "tp"),
    )
    return jax.shard_map(
        on_device,
        mesh=mesh,
        in_specs=placed,
        out_specs=P(("groups", "pool"), "tp"),
        check_vma=False,
    )
```

profile of v0, /device:TPU:1, one launch (start us, length us, event | category | flops | bytes accessed | tf_op | source)
XLA Modules:
  0.0 227.8 jit_solution(9095619187333805453)
XLA Ops:
  6.5 0.0 copy-start.5
  6.5 0.0 copy-start.4
  6.5 0.9 slice_convert_fusion
  7.4 1.2 fusion.23
  8.6 2.1 fusion.36
  10.8 0.0 copy-done.4
  10.8 0.3 fusion.18
  11.1 0.0 copy-done.5
  11.1 0.5 fusion.13
  11.6 0.2 reshape.17
  11.8 21.0 %all-gather = bf16[4,6,16384]{2,1,0:T(8,128)(2,1)S(1)} all-gather(bf16[1,6,16384]{2,1,0:T(8,128)(2,1)S(1)} %reshape.17), channel_id=1, replica_groups=mesh['groups'=2,'pool'=4,'tp'=4] {'tp'}, dimensions={0}, use_global_device_ids=true | all-gather | bytes 983040 | tf_op jit(solution)/shard_map/all_gather | solution.py:61
  32.8 1.1 all_to_all.14
  33.9 1.3 copy.12
  35.2 6.7 %all-to-all-start = ((bf16[24,4,4096]{2,0,1:T(8,128)(2,1)}), bf16[24,4,4096]{2,0,1:T(8,128)(2,1)S(1)}, u32[]{:S(2)}, u32[]{:S(2)}) async-start(bf16[24,4,4096]{2,0,1:T(8,128)(2,1)} %copy.12), calls=%async_computation | async-start | bytes 1572864 | tf_op jit(solution)/shard_map/all_to_all | solution.py:62
  41.9 0.0 all-reduce.4.cloned.1.call-start
  41.9 10.8 %all-to-all-done = bf16[24,4,4096]{2,0,1:T(8,128)(2,1)S(1)} async-done(((bf16[24,4,4096]{2,0,1:T(8,128)(2,1)}), bf16[24,4,4096]{2,0,1:T(8,128)(2,1)S(1)}, u32[]{:S(2)}, u32[]{:S(2)}) %all-to-all-start) | async-done | bytes 786464 | tf_op jit(solution)/shard_map/all_to_all | solution.py:62
  52.7 0.0 copy-start.2
  52.7 0.0 copy-start.3
  52.7 7.6 %fusion.37 = f32[96,1792]{1,0:T(8,128)S(1)} fusion(bf16[96,4096]{1,0:T(8,128)(2,1)S(1)} %bitcast.36, bf16[4096,1792]{1,0:T(8,128)(2,1)} %param.15), kind=kOutput, calls=%fused_computation.45 | convolution fusion | flops 1409286144 | bytes 16154624 | tf_op jit(solution)/shard_map/dot_general | solution.py:66
  60.4 0.0 copy-done.2
  60.4 0.0 copy-start.1
  60.4 0.8 copy-done.1
  61.3 0.0 all-reduce.4.cloned.1.call-update
  61.3 0.0 all-reduce.6.cloned.1.call-start
  61.3 0.0 copy-done.3
  61.4 32.2 %all-reduce.4.cloned.1.call-done = f32[96,1792]{1,0:T(8,128)} async-done(((f32[96,1792]{1,0:T(8,128)}), f32[96,1792]{1,0:T(8,128)}) %all-reduce.4.cloned.1.call-update) | async-done | bytes 688144 | tf_op jit(solution)/shard_map/psum | solution.py:71
  93.6 0.0 copy-start
  93.6 9.6 %convolution_convert_fusion = bf16[96,4608]{1,0:T(8,128)(2,1)} fusion(bf16[1792,4608]{1,0:T(8,128)(2,1)} %param.18, f32[96,1792]{1,0:T(8,128)} %all-reduce.4.cloned.1.call-done, f32[1792]{0:T(1024)S(1)} %convert_element_type.65), kind=kOutput, calls=%fused_computation | convolution fusion | flops 1586233344 | bytes 18095104 | tf_op jit(solution)/shard_map/dot_general | solution.py:76
  103.2 0.0 copy-done
  103.2 9.4 %convolution_convert_fusion.1 = bf16[96,4608]{1,0:T(8,128)(2,1)} fusion(bf16[1792,4608]{1,0:T(8,128)(2,1)} %param.17, f32[96,1792]{1,0:T(8,128)S(1)} %copy-done, f32[1792]{0:T(1024)S(1)} %convert_element_type.65), kind=kOutput, calls=%fused_computation.1 | convolution fusion | flops 1586233344 | bytes 18095104 | tf_op jit(solution)/shard_map/dot_general | solution.py:75
  112.6 0.0 all-reduce.6.cloned.1.call-update
  112.6 0.0 reduce-scatter.2.cloned.1.call-start
  112.6 0.1 multiply_reduce_fusion
  112.8 10.5 %psum.30 = bf16[96]{0:T(256)(128)(2,1)S(1)} all-reduce(bf16[96]{0:T(256)(128)(2,1)S(1)} %multiply_reduce_fusion), channel_id=1, replica_groups=mesh['groups'=2,'pool'=4,'tp'=4] {'tp'}, use_global_device_ids=true, to_apply=%region_5.6 | all-reduce | flops 96 | bytes 384 | tf_op jit(solution)/shard_map/psum | solution.py:80
  123.3 65.8 %all-reduce.6.cloned.1.call-done = (bf16[96,4608]{1,0:T(8,128)(2,1)}, bf16[96,4608]{1,0:T(8,128)(2,1)}) async-done(((bf16[96,4608]{1,0:T(8,128)(2,1)}, bf16[96,4608]{1,0:T(8,128)(2,1)}), (bf16[96,4608]{1,0:T(8,128)(2,1)}, bf16[96,4608]{1,0:T(8,128)(2,1)})) %all-reduce.6.cloned.1.call-update) | async-done | bytes 1769488 | tf_op jit(solution)/shard_map/psum | solution.py:79
  189.1 9.9 %convolution_convert_fusion.2 = bf16[96,1792]{1,0:T(8,128)(2,1)} fusion(bf16[4608,1792]{1,0:T(8,128)(2,1)} %param.19, bf16[96,4608]{1,0:T(8,128)(2,1)} %get-tuple-element.5, bf16[96,4608]{1,0:T(8,128)(2,1)} %get-tuple-element.6, f32[96]{0:T(128)S(1)} %add_rsqrt_fusion), kind=kOutput, calls=%fused_computation.2 | convolution fusion | flops 1590042624 | bytes 18628992 | tf_op jit(solution)/shard_map/dot_general | solution.py:87
  199.0 0.0 reduce-scatter.2.cloned.1.call-update
  199.0 20.7 %reduce-scatter.2.cloned.1.call-done = bf16[24,1792]{1,0:T(8,128)(2,1)} async-done(((bf16[96,1792]{1,0:T(8,128)(2,1)}), bf16[24,1792]{1,0:T(8,128)(2,1)}) %reduce-scatter.2.cloned.1.call-update) | async-done | bytes 86032 | tf_op jit(solution)/shard_map/reduce_scatter | solution.py:86
  219.7 1.5 add_convert_fusion
  (5 shorter events, 0.1 us)
Async XLA Ops:
  6.5 4.6 %copy-start.5 = (bf16[6,512,512]{2,1,0:T(8,128)(2,1)S(1)}, bf16[6,512,512]{2,1,0:T(8,128)(2,1)}, u32[]{:S(2)}) copy-start(bf16[6,512,512]{2,1,0:T(8,128)(2,1)} %param.11) | copy-start | bytes 9437188
  6.5 4.2 %copy-start.4 = (s32[6]{0:T(128)S(1)}, s32[6]{0:T(128)}, u32[]{:S(2)}) copy-start(s32[6]{0:T(128)} %param.13) | copy-start | bytes 76
  35.2 17.5 %all-to-all-start = ((bf16[24,4,4096]{2,0,1:T(8,128)(2,1)}), bf16[24,4,4096]{2,0,1:T(8,128)(2,1)S(1)}, u32[]{:S(2)}, u32[]{:S(2)}) async-start(bf16[24,4,4096]{2,0,1:T(8,128)(2,1)} %copy.12), calls=%async_computation | async-start | bytes 1572864 | tf_op jit(solution)/shard_map/all_to_all | solution.py:62
  41.9 51.6 %all-reduce.4.cloned.1.call-start = ((), (), s32[]{:S(2)}) async-start(), calls=%async_computation.2 | async-start | bytes 1376256 | tf_op jit(solution)/shard_map/psum | solution.py:71
  52.7 7.6 %copy-start.2 = (bf16[24,1792]{1,0:T(8,128)(2,1)S(1)}, bf16[24,1792]{1,0:T(8,128)(2,1)}, u32[]{:S(2)}) copy-start(bf16[24,1792]{1,0:T(8,128)(2,1)} %param.14) | copy-start | bytes 258052
  52.7 8.6 %copy-start.3 = (bf16[1792]{0:T(1024)(128)(2,1)S(1)}, bf16[1792]{0:T(1024)(128)(2,1)}, u32[]{:S(2)}) copy-start(bf16[1792]{0:T(1024)(128)(2,1)} %param.16) | copy-start | bytes 10756
  60.4 0.8 copy-start.1
  61.3 127.8 %all-reduce.6.cloned.1.call-start = ((), (), s32[]{:S(2)}) async-start(), calls=%async_computation.4 | async-start | bytes 3538944 | tf_op jit(solution)/shard_map/psum | solution.py:79
  93.6 9.6 %copy-start = (f32[96,1792]{1,0:T(8,128)S(1)}, f32[96,1792]{1,0:T(8,128)}, u32[]{:S(2)}) copy-start(f32[96,1792]{1,0:T(8,128)} %all-reduce.4.cloned.1.call-done) | copy-start | bytes 2064388
  112.6 107.1 %reduce-scatter.2.cloned.1.call-start = ((), (), s32[]{:S(2)}) async-start(), calls=%async_computation.3 | async-start | bytes 430080 | tf_op jit(solution)/shard_map/reduce_scatter | solution.py:86
Sparse Core Ops, SparseCore 0:
  61.4 32.1 all-reduce.3
  112.7 76.3 all-reduce.5
  199.2 20.5 reduce-scatter.1
where the time goes:
time: 229 us; the launch traced here: 228 us
  waiting for transfers between devices  130 us (57%)
  matrix products  40.3 us (18%)
  blocking collectives  31.5 us (14%)
  between operations  13.2 us (6%)
  starting transfers between devices  6.8 us (3%)
  local copies, waits for them, and re-layouts  3.5 us (2%)
  other arithmetic  2.92 us (1%)
    psum x1, waiting for transfers between devices, finish_rows(): lax.psum(up_part.astype(jnp.bfloat16), 'tp').astype(jnp.float32)  65.8 us
    psum x1, waiting for transfers between devices, finish_rows(): post_attn = lax.psum(summand, 'pool')  32.2 us
    all_gather x1, blocking collectives, finish_rows(): columns = lax.all_gather(attended, 'tp', axis=0, tiled=True)  21 us
    reduce_scatter x1, waiting for transfers between devices, finish_rows(): lax.psum_scatter(jnp.dot(hidden, down_weight, preferred_element_type=jnp....  20.7 us
    all_to_all x1, waiting for transfers between devices, finish_rows(): lax.all_to_all(columns, 'pool', split_axis=1, concat_axis=0, tiled=True)  10.8 us
    psum x1, blocking collectives, finish_rows(): lax.psum(squares.astype(jnp.bfloat16), 'tp').astype(jnp.float32)  10.5 us
    dot_general x1, matrix products, finish_rows(): jnp.dot(hidden, down_weight, preferred_element_type=jnp.float32)  9.94 us
    dot_general x1, matrix products, finish_rows(): up_part = jnp.dot(scaled, up_weight, preferred_element_type=jnp.float32)  9.62 us
  transfers between devices with their start and end apart: 4, of which 4 were waited for; matrix products, arithmetic and copies ran while one was open for 0% of the time, Pallas kernels for 0%

commit v1 on v0

v1 whole, which is shorter than its diff:
```python
import functools
import math

import jax
import jax.numpy as jnp
import numpy as np
from jax import lax
from jax.experimental import pallas as pl
from jax.experimental.pallas import tpu as pltpu
from jax.sharding import PartitionSpec as P

D = 7168
HEADS = 64
HD = 256


epsilon = 1e-06


def attend(queries, cached_entries, new_entry, lengths):
    amount = queries.shape[0]
    query_heads = queries.reshape(amount, HEADS, HD)
    key_rows = cached_entries[:, :, :HD]
    value_rows = cached_entries[:, :, HD:]
    factor = 1.0 / math.sqrt(HD)
    scores = (
        jnp.einsum("rhd,rld->rhl", query_heads, key_rows, preferred_element_type=jnp.float32)
        * factor
    )
    own_score = (
        jnp.einsum("rhd,rd->rh", query_heads, new_entry[:, :HD], preferred_element_type=jnp.float32)
        * factor
    )
    positions = lax.broadcasted_iota(jnp.int32, scores.shape, 2)
    usable = positions < lengths[:, None, None]
    scores = jnp.where(usable, scores, -jnp.inf)
    peak_score = jnp.maximum(jnp.max(scores, axis=2), own_score)
    weights_raw = jnp.where(usable, jnp.exp(scores - peak_score[:, :, None]), 0.0)
    own_raw = jnp.exp(own_score - peak_score)
    totals = jnp.sum(weights_raw, axis=2) + own_raw
    weights = (weights_raw / totals[:, :, None]).astype(jnp.bfloat16)
    own_weight = (own_raw / totals).astype(jnp.bfloat16)
    mixture = jnp.einsum("rhl,rld->rhd", weights, value_rows, preferred_element_type=jnp.float32)
    mixture = mixture + own_weight.astype(jnp.float32)[:, :, None] * new_entry[:, None, HD:].astype(
        jnp.float32
    )
    return mixture.reshape(amount, HEADS * HD).astype(jnp.bfloat16)


PAD = 8
LAG = 2
SLOTS = 8
MESH = pl.DeviceIdType.MESH


def tile_of(extent):
    return 256 if extent % 256 == 0 else 128


def layer_kernel(
    pools,
    tps,
    att,
    resid,
    gain,
    pick_local,
    pick_all,
    wo_hbm,
    wg_hbm,
    wu_hbm,
    wd_hbm,
    out,
    wo,
    wg,
    wu,
    wd,
    raw,
    stage,
    slabs,
    x,
    pf,
    psend,
    precv,
    drecv,
    own_post,
    scl,
    sq_all,
    sq,
    sq_recv,
    s_in,
    part,
    sbuf,
    rbuf,
    hid,
    acc,
    w_sem,
    g_sem,
    u_sem,
    a_send,
    a_recv,
    c_right,
    c_left,
    c_recv,
    p_send,
    p_recv,
    s_send,
    s_recv,
    q_send,
    q_recv,
    e_send,
    e_recv,
    r_send,
    r_recv,
    h_send,
    h_recv,
    d_send,
    d_recv,
):
    p = lax.axis_index("pool")
    t = lax.axis_index("tp")
    block = resid.shape[0]
    width = resid.shape[1]
    pad, cols = att.shape[1], att.shape[2]
    slab_rows = slabs.shape[1]
    rows = x.shape[0]
    tile = part.shape[3]
    tiles = part.shape[0]
    pairs = (tiles + 1) // 2
    slots = wg.shape[0]
    out_tile = tile_of(width)
    last = tps - 1
    before, behind = lax.rem(t + tps - 1, tps), lax.rem(t + 1, tps)

    def weight_copies(j):
        slot = lax.rem(j, slots)
        at = pl.ds(pl.multiple_of(j * tile, tile), tile)
        return (
            pltpu.make_async_copy(wg_hbm.at[:, at], wg.at[slot], g_sem.at[slot]),
            pltpu.make_async_copy(wu_hbm.at[:, at], wu.at[slot], u_sem.at[slot]),
        )

    wo_copy = pltpu.make_async_copy(wo_hbm, wo, w_sem.at[0])
    wd_copy = pltpu.make_async_copy(wd_hbm, wd, w_sem.at[1])
    wo_copy.start()

    barrier = pltpu.get_barrier_semaphore()
    for k in range(1, pools):
        pl.semaphore_signal(
            barrier, inc=1, device_id={"pool": lax.rem(p + k, pools)}, device_id_type=MESH
        )

    @pl.when(t > 0)
    def _():
        pl.semaphore_signal(barrier, inc=1, device_id={"tp": before}, device_id_type=MESH)

    @pl.when(t < last)
    def _():
        pl.semaphore_signal(barrier, inc=1, device_id={"tp": behind}, device_id_type=MESH)

    peers = pools - 1 + lax.convert_element_type(t > 0, jnp.int32)
    pl.semaphore_wait(barrier, peers + lax.convert_element_type(t < last, jnp.int32))

    def remote(src, dst, send, recv, device):
        return pltpu.make_async_remote_copy(
            src_ref=src,
            dst_ref=dst,
            send_sem=send,
            recv_sem=recv,
            device_id=device,
            device_id_type=MESH,
        )

    def pool_peer(k):
        return lax.rem(p + k, pools)

    def att_copy(k):
        q = pool_peer(k)
        return remote(att.at[q], raw.at[p], a_send.at[k], a_recv.at[p], {"pool": q})

    def att_arrival(k):
        q = pool_peer(k)
        return remote(att.at[q], raw.at[q], a_send.at[k], a_recv.at[q], {"pool": q})

    for k in range(1, pools):
        att_copy(k).start()

    for j in range(min(slots, tiles)):
        for copy in weight_copies(jnp.int32(j)):
            copy.start()
    wd_copy.start()

    stage[pl.ds(pl.multiple_of(p * pad, 8), pad), :] = att[p].astype(jnp.float32)
    for k in range(1, pools):
        att_arrival(k).wait_recv()
        q = pool_peer(k)
        stage[pl.ds(pl.multiple_of(q * pad, 8), pad), :] = raw[q].astype(jnp.float32)
    slabs[t] = jnp.dot(
        pick_local[...],
        stage[pl.ds(0, pools * pad), :].astype(jnp.bfloat16),
        preferred_element_type=jnp.float32,
    ).astype(jnp.bfloat16)

    def slab_right(origin):
        return remote(
            slabs.at[origin], slabs.at[origin], c_right.at[origin], c_recv.at[origin], {"tp": behind}
        )

    def slab_left(origin):
        return remote(
            slabs.at[origin], slabs.at[origin], c_left.at[origin], c_recv.at[origin], {"tp": before}
        )

    @pl.when(t < last)
    def _():
        slab_right(t).start()

    @pl.when(t > 0)
    def _():
        slab_left(t).start()

    for k in range(1, tps):

        @pl.when(t - k >= 0)
        def _():
            slab_left(t - k).wait_recv()

            @pl.when(t < last)
            def _():
                slab_right(t - k).start()

        @pl.when(t + k <= last)
        def _():
            slab_right(t + k).wait_recv()

            @pl.when(t > 0)
            def _():
                slab_left(t + k).start()

    for origin in range(tps):
        stage[pl.ds(origin * slab_rows, slab_rows), :] = slabs[origin].astype(jnp.float32)
    step_cols = tile_of(cols)

    @pl.loop(0, cols // step_cols)
    def _(n):
        at = pl.ds(pl.multiple_of(n * step_cols, step_cols), step_cols)
        x[:, at] = jnp.dot(
            pick_all[...],
            stage[pl.ds(0, rows), at].astype(jnp.bfloat16),
            preferred_element_type=jnp.float32,
        ).astype(jnp.bfloat16)

    wo_copy.wait()

    @pl.loop(0, width // out_tile)
    def _(n):
        at = pl.ds(pl.multiple_of(n * out_tile, out_tile), out_tile)
        value = jnp.dot(x[...], wo[:, at], preferred_element_type=jnp.float32)
        pf[:, at] = value
        for q in range(pools):
            psend[q, :, at] = value[q * block : (q + 1) * block].astype(jnp.bfloat16)

    def part_copy(k):
        q = pool_peer(k)
        return remote(psend.at[q], precv.at[p], p_send.at[k], p_recv.at[p], {"pool": q})

    def part_arrival(k):
        q = pool_peer(k)
        return remote(psend.at[q], precv.at[q], p_send.at[k], p_recv.at[q], {"pool": q})

    for k in range(1, pools):
        part_copy(k).start()
    post = pf[pl.ds(pl.multiple_of(p * block, 8), block), :] + resid[...].astype(jnp.float32)
    for k in range(1, pools):
        part_arrival(k).wait_recv()
        post = post + precv[pool_peer(k)].astype(jnp.float32)
    own_post[...] = post
    scl[p] = (post * gain[...]).astype(jnp.bfloat16)
    sq_all[p] = jnp.broadcast_to(jnp.sum(post * post, axis=1, keepdims=True), (block, 128))

    def scaled_copy(k):
        q = pool_peer(k)
        return remote(scl.at[p], scl.at[p], s_send.at[k], s_recv.at[p], {"pool": q})

    def scaled_arrival(k):
        q = pool_peer(k)
        return remote(scl.at[q], scl.at[q], s_send.at[k], s_recv.at[q], {"pool": q})

    def square_copy(k):
        q = pool_peer(k)
        return remote(sq_all.at[p], sq_all.at[p], q_send.at[k], q_recv.at[p], {"pool": q})

    def square_arrival(k):
        q = pool_peer(k)
        return remote(sq_all.at[q], sq_all.at[q], q_send.at[k], q_recv.at[q], {"pool": q})

    for k in range(1, pools):
        square_copy(k).start()
        scaled_copy(k).start()
    for k in range(1, pools):
        square_arrival(k).wait_recv()
        scaled_arrival(k).wait_recv()
    for q in range(pools):
        pf[pl.ds(q * block, block), :] = scl[q].astype(jnp.float32)
        for s in range(2):
            sq[s, pl.ds(q * block, block), :] = sq_all[q]
    s_in[...] = pf[...].astype(jnp.bfloat16)
    acc[...] = jnp.zeros_like(acc)

    def lanes(s):
        if s == 0:
            return last - t, before, behind
        return t, behind, before

    def square_hop(s):
        _, after, _ = lanes(s)
        return remote(sq.at[s], sq_recv.at[s], e_send.at[s], e_recv.at[s], {"tp": after})

    def sum_hop(s, j):
        _, after, _ = lanes(s)
        return remote(sbuf.at[j], rbuf.at[j], r_send.at[j], r_recv.at[j], {"tp": after})

    def hidden_hop(s, j):
        _, _, back = lanes(s)
        return remote(hid.at[j], hid.at[j], h_send.at[j], h_recv.at[j], {"tp": back})

    def down(j):
        piece = hid[j]
        at = pl.ds(pl.multiple_of(j * tile, tile), tile)

        @pl.loop(0, width // out_tile)
        def _(n):
            here = pl.ds(pl.multiple_of(n * out_tile, out_tile), out_tile)
            acc[:, here] += jnp.dot(piece, wd[at, here], preferred_element_type=jnp.float32)

    wd_copy.wait()

    def one_step(i):
        for s in range(2):
            j = 2 * i + s

            @pl.when(j < tiles)
            def _():
                slot = lax.rem(j, slots)
                for copy in weight_copies(j):
                    copy.wait()
                part[j, 0] = jnp.dot(s_in[...], wg[slot], preferred_element_type=jnp.float32)
                part[j, 1] = jnp.dot(s_in[...], wu[slot], preferred_element_type=jnp.float32)

                @pl.when(j + slots < tiles)
                def _():
                    for copy in weight_copies(j + slots):
                        copy.start()

        for s in range(2):
            far, _, _ = lanes(s)
            c = i - LAG * far
            j = 2 * c + s

            @pl.when((c >= 0) & (j < tiles))
            def _():
                @pl.when(far > 0)
                def _():
                    @pl.when(c == 0)
                    def _():
                        square_hop(s).wait_recv()
                        sq[s] = sq[s] + sq_recv[s]

                    sum_hop(s, j).wait_recv()
                    part[j] = part[j] + rbuf[j].astype(jnp.float32)

                @pl.when(far < last)
                def _():
                    @pl.when(c == 0)
                    def _():
                        square_hop(s).start()

                    sbuf[j] = part[j].astype(jnp.bfloat16)
                    sum_hop(s, j).start()

                @pl.when(far == last)
                def _():
                    inv = lax.rsqrt(sq[s][:, :1] / D + epsilon)
                    gate = part[j, 0] * inv
                    up = part[j, 1] * inv
                    hid[j] = (gate / (1.0 + jnp.exp(-gate)) * up).astype(jnp.bfloat16)
                    if tps > 1:
                        hidden_hop(s, j).start()
                    down(j)

        for s in range(2):
            far, _, _ = lanes(s)
            back = last - far
            c = i - LAG * last - LAG * back
            j = 2 * c + s

            @pl.when((back > 0) & (c >= 0) & (j < tiles))
            def _():
                hidden_hop(s, j).wait_recv()

                @pl.when(back < last)
                def _():
                    hidden_hop(s, j).start()

                down(j)

    pl.loop(0, pairs + 2 * LAG * last)(one_step)

    for k in range(1, pools):
        part_copy(k).wait_send()

    @pl.loop(0, width // out_tile)
    def _(n):
        at = pl.ds(pl.multiple_of(n * out_tile, out_tile), out_tile)
        value = acc[:, at]
        for q in range(pools):
            psend[q, :, at] = value[q * block : (q + 1) * block].astype(jnp.bfloat16)

    def down_copy(k):
        q = pool_peer(k)
        return remote(psend.at[q], drecv.at[p], d_send.at[k], d_recv.at[p], {"pool": q})

    def down_arrival(k):
        q = pool_peer(k)
        return remote(psend.at[q], drecv.at[q], d_send.at[k], d_recv.at[q], {"pool": q})

    for k in range(1, pools):
        down_copy(k).start()
    total = own_post[...] + acc[pl.ds(pl.multiple_of(p * block, 8), block), :]
    for k in range(1, pools):
        down_arrival(k).wait_recv()
        total = total + drecv[pool_peer(k)].astype(jnp.float32)
    out[...] = total.astype(jnp.bfloat16)

    for k in range(1, pools):
        att_copy(k).wait_send()
        scaled_copy(k).wait_send()
        square_copy(k).wait_send()
        down_copy(k).wait_send()
    for origin in range(tps):

        @pl.when((t < last) & (origin <= t))
        def _():
            slab_right(origin).wait_send()

        @pl.when((t > 0) & (origin >= t))
        def _():
            slab_left(origin).wait_send()

    for s in range(2):
        far, _, _ = lanes(s)

        @pl.when(far < last)
        def _():
            square_hop(s).wait_send()

    @pl.loop(0, pairs)
    def _(c):
        for s in range(2):
            far, _, _ = lanes(s)
            j = 2 * c + s

            @pl.when((far < last) & (j < tiles))
            def _():
                sum_hop(s, j).wait_send()

            @pl.when((far > 0) & (j < tiles))
            def _():
                hidden_hop(s, j).wait_send()


def finish_rows(att, resid, gain, out_weight, gate_weight, up_weight, down_weight, amount):
    pools, tps = lax.axis_size("pool"), lax.axis_size("tp")
    block, width = resid.shape
    pad, cols = att.shape[1], att.shape[2]
    ff = gate_weight.shape[1]
    slab_rows = pools * amount
    rows = slab_rows * tps
    tile = tile_of(ff)
    tiles = ff // tile
    slots = min(SLOTS, tiles)

    local = np.arange(slab_rows)
    pick_local = np.zeros((slab_rows, pools * pad), np.float32)
    pick_local[local, local // amount * pad + local % amount] = 1
    every = np.arange(rows)
    of_pool, of_tp, of_row = every // block, every // amount % tps, every % amount
    pick_all = np.zeros((rows, rows), np.float32)
    pick_all[every, (of_tp * pools + of_pool) * amount + of_row] = 1

    vmem = pl.BlockSpec(memory_space=pltpu.VMEM)
    anywhere = pl.BlockSpec(memory_space=pl.ANY)
    bf16, f32 = jnp.bfloat16, jnp.float32
    dma = pltpu.SemaphoreType.DMA
    scratch = [
        pltpu.VMEM(out_weight.shape, bf16),
        pltpu.VMEM((slots, gate_weight.shape[0], tile), bf16),
        pltpu.VMEM((slots, gate_weight.shape[0], tile), bf16),
        pltpu.VMEM(down_weight.shape, bf16),
        pltpu.VMEM((pools, pad, cols), bf16),
        pltpu.VMEM((max(rows, pools * pad), cols), f32),
        pltpu.VMEM((tps, slab_rows, cols), bf16),
        pltpu.VMEM((rows, cols), bf16),
        pltpu.VMEM((rows, width), f32),
        pltpu.VMEM((pools, block, width), bf16),
        pltpu.VMEM((pools, block, width), bf16),
        pltpu.VMEM((pools, block, width), bf16),
        pltpu.VMEM((block, width), f32),
        pltpu.VMEM((pools, block, width), bf16),
        pltpu.VMEM((pools, block, 128), f32),
        pltpu.VMEM((2, rows, 128), f32),
        pltpu.VMEM((2, rows, 128), f32),
        pltpu.VMEM((rows, width), bf16),
        pltpu.VMEM((tiles, 2, rows, tile), f32),
        pltpu.VMEM((tiles, 2, rows, tile), bf16),
        pltpu.VMEM((tiles, 2, rows, tile), bf16),
        pltpu.VMEM((tiles, rows, tile), bf16),
        pltpu.VMEM((rows, width), f32),
        dma((2,)),
        dma((slots,)),
        dma((slots,)),
        dma((pools,)),
        dma((pools,)),
        dma((tps,)),
        dma((tps,)),
        dma((tps,)),
        dma((pools,)),
        dma((pools,)),
        dma((pools,)),
        dma((pools,)),
        dma((pools,)),
        dma((pools,)),
        dma((2,)),
        dma((2,)),
        dma((tiles,)),
        dma((tiles,)),
        dma((tiles,)),
        dma((tiles,)),
        dma((pools,)),
        dma((pools,)),
    ]
    return pl.pallas_call(
        functools.partial(layer_kernel, pools, tps),
        out_shape=jax.ShapeDtypeStruct((block, width), bf16),
        in_specs=[vmem] * 5 + [anywhere] * 4,
        out_specs=vmem,
        scratch_shapes=scratch,
        compiler_params=pltpu.CompilerParams(
            collective_id=0, has_side_effects=True, vmem_limit_bytes=62 << 20
        ),
        name="layer",
    )(
        att,
        resid,
        gain,
        jnp.asarray(pick_local, bf16),
        jnp.asarray(pick_all, bf16),
        out_weight,
        gate_weight,
        up_weight,
        down_weight,
    )


def on_device(
    queries,
    cached_entries,
    new_entry,
    lengths,
    residual,
    out_weight,
    norm_gain,
    gate_weight,
    up_weight,
    down_weight,
):
    pools = lax.axis_size("pool")
    amount = queries.shape[0]
    pad = -(-amount // PAD) * PAD
    attended = attend(queries, cached_entries, new_entry, lengths)
    att = attended.reshape(amount, pools, -1).transpose(1, 0, 2)
    att = jnp.pad(att, ((0, 0), (0, pad - amount), (0, 0)))
    return finish_rows(
        att,
        residual,
        norm_gain.astype(jnp.float32)[None, :],
        out_weight,
        gate_weight,
        up_weight,
        down_weight,
        amount,
    )


def solution(mesh):
    placed = (
        P(("groups", "pool", "tp"), None),
        P(("groups", "pool", "tp"), None, None),
        P(("groups", "pool", "tp"), None),
        P(("groups", "pool", "tp")),
        P(("groups", "pool"), "tp"),
        P("pool", "tp"),
        P("tp"),
        P("tp", "pool"),
        P("tp", "pool"),
        P("pool", "tp"),
    )
    return jax.shard_map(
        on_device,
        mesh=mesh,
        in_specs=placed,
        out_specs=P(("groups", "pool"), "tp"),
        check_vma=False,
    )
```

time: 229 us -> 107 us (0.47)
  waiting for transfers between devices: 130 us -> 0 us
  Pallas kernels: 0 us -> 98.3 us
  matrix products: 40.3 us -> 3.81 us
  blocking collectives: 31.5 us -> 0 us
  between operations: 13.2 us -> 0.06 us
  starting transfers between devices: 6.8 us -> 0 us
    pallas_call x0 -> x1, Pallas kernels: none -> 98.3 us  [finish_rows(): pl.pallas_call(functools.partial(layer_kernel, pools, tps), out_shape=jax...]
    psum x2 -> x0, waiting for transfers between devices: 98 us -> none  [the longest x1 65.8 us: finish_rows(): lax.psum(up_part.astype(jnp.bfloat16), 'tp').astype(jnp.float32)]
    dot_general x4 -> x0, matrix products: 36.6 us -> none  [the longest x1 9.94 us: finish_rows(): jnp.dot(hidden, down_weight, preferred_element_type=jnp.float32)]
    all_gather x1 -> x0, blocking collectives: 21 us -> none  [finish_rows(): columns = lax.all_gather(attended, 'tp', axis=0, tiled=True)]
    reduce_scatter x1 -> x0, waiting for transfers between devices: 20.7 us -> none  [finish_rows(): lax.psum_scatter(jnp.dot(hidden, down_weight, preferred_element_type=jnp....]
    all_to_all x1 -> x0, waiting for transfers between devices: 10.8 us -> none  [finish_rows(): lax.all_to_all(columns, 'pool', split_axis=1, concat_axis=0, tiled=True)]
    psum x1 -> x0, blocking collectives: 10.5 us -> none  [finish_rows(): lax.psum(squares.astype(jnp.bfloat16), 'tp').astype(jnp.float32)]
    all_to_all x1 -> x0, starting transfers between devices: 6.71 us -> none  [finish_rows(): lax.all_to_all(columns, 'pool', split_axis=1, concat_axis=0, tiled=True)]
  transfers between devices with their start and end apart: 4 -> 0, of which waited for: 4 -> 0; matrix products, arithmetic and copies ran while one was open for 0% -> 0% of each run, Pallas kernels for 0% -> 0%
where the time goes in v1:
time: 107 us; the launch traced here: 106 us
  Pallas kernels  98.3 us (92%)
  matrix products  3.81 us (4%)
  local copies, waits for them, and re-layouts  3.13 us (3%)
    pallas_call x1, Pallas kernels, finish_rows(): pl.pallas_call(functools.partial(layer_kernel, pools, tps), out_shape=jax...  98.3 us
    dot_general x1, matrix products, attend(): jnp.einsum('rhd,rld->rhl', query_heads, key_rows, preferred_element_type=...  2.26 us

profile of v1, /device:TPU:1, one launch (start us, length us, event | category | flops | bytes accessed | tf_op | source)
XLA Modules:
  0.0 106.4 jit_solution(4881019908887843183)
XLA Ops:
  0.0 0.0 copy-start.2
  0.0 0.0 copy-start.1
  0.0 2.3 %fusion.33 = (f32[6,64]{1,0:T(8,128)S(1)}, f32[6,64,512]{2,1,0:T(8,128)S(1)}) fusion(bf16[6,512,512]{2,1,0:T(8,128)(2,1)} %param.13, bf16[1,6,64,256]{3,1,2,0:T(8,128)(2,1)} %bitcast.32, s32[6]{0:T(128)} %param.15), kind=kOutput, calls=%fused_computation.33 | convolution fusion | flops 101449344 | bytes 2623488 | tf_op jit(solution)/shard_map/rhd,rld->rhl/dot_general | solution.py:27
  2.3 0.7 slice_convert_fusion
  3.0 1.1 %fusion.21 = f32[6,1,64]{2,1,0:T(1,128)S(1)} fusion(bf16[1,6,64,256]{3,1,2,0:T(8,128)(2,1)} %bitcast.33, bf16[6,256,1]{1,0,2:T(8,128)(2,1)S(1)} %get-tuple-element.8), kind=kOutput, calls=%fused_computation.17 | convolution fusion | flops 196608 | bytes 201216 | tf_op jit(solution)/shard_map/rhd,rd->rh/dot_general | solution.py:31
  4.1 0.0 copy-done.1
  4.1 0.3 fusion.16
  4.4 0.0 copy-done.2
  4.4 0.0 copy-start
  4.5 0.4 fusion.13
  4.9 0.1 convert_element_type.28
  5.0 0.1 copy.47
  5.2 0.7 pad.4.att
  5.9 0.0 copy-done
  5.9 0.6 reshape.14.gain
  6.5 98.3 %layer.1 = bf16[24,1792]{1,0:T(8,128)(2,1)} custom-call(bf16[4,8,4096]{2,1,0:T(8,128)(2,1)} %pad.4.att, bf16[24,1792]{1,0:T(8,128)(2,1)} %resid.1, f32[1,1792]{1,0:T(1,128)} %reshape.14.gain, bf16[24,32]{1,0:T(8,128)(2,1)} %constant.14.clone.pick_local, bf16[96,96]{1,0:T(8,128)(2,1)} %constant.15.clone.pick_all, bf16[4096,1792]{1,0:T(8,128)(2,1)} %wo_hbm.1, ...), custom_call_target="tpu_custom_call" | custom-call | tf_op jit(solution)/shard_map/layer/pallas_call | solution.py:541
  104.8 1.5 %copy.49 = bf16[24,1792]{1,0:T(8,128)(2,1)} copy(bf16[24,1792]{1,0:T(8,128)(2,1)} %layer.1) | data formatting | bytes 172032
  (2 shorter events, 0.0 us)
Async XLA Ops:
  0.0 4.4 %copy-start.2 = (bf16[6,512,512]{2,1,0:T(8,128)(2,1)S(1)}, bf16[6,512,512]{2,1,0:T(8,128)(2,1)}, u32[]{:S(2)}) copy-start(bf16[6,512,512]{2,1,0:T(8,128)(2,1)} %param.13) | copy-start | bytes 9437188
  0.0 4.1 %copy-start.1 = (s32[6]{0:T(128)S(1)}, s32[6]{0:T(128)}, u32[]{:S(2)}) copy-start(s32[6]{0:T(128)} %param.15) | copy-start | bytes 76
  4.4 1.5 %copy-start = (bf16[1792]{0:T(1024)(128)(2,1)S(1)}, bf16[1792]{0:T(1024)(128)(2,1)}, u32[]{:S(2)}) copy-start(bf16[1792]{0:T(1024)(128)(2,1)} %param.18) | copy-start | bytes 10756

commit v2 on v1

--- a/solution.py
+++ b/solution.py
@@ -351,7 +351,6 @@
                     for copy in weight_copies(j + slots):
                         copy.start()
 
-        for s in range(2):
             far, _, _ = lanes(s)
             c = i - LAG * far
             j = 2 * c + s

time: 107 us -> 107 us (level)
  no operation moved by 1% of the time
where the time goes in v2:
time: 107 us; the launch traced here: 106 us
  Pallas kernels  98.3 us (92%)
  matrix products  3.81 us (4%)
  local copies, waits for them, and re-layouts  3.13 us (3%)
    pallas_call x1, Pallas kernels, finish_rows(): pl.pallas_call(functools.partial(layer_kernel, pools, tps), out_shape=jax...  98.3 us
    dot_general x1, matrix products, attend(): jnp.einsum('rhd,rld->rhl', query_heads, key_rows, preferred_element_type=...  2.26 us

profile of v2, /device:TPU:1, one launch (start us, length us, event | category | flops | bytes accessed | tf_op | source)
XLA Modules:
  0.0 106.4 jit_solution(1167742692584827824)
XLA Ops:
  0.0 0.0 copy-start.2
  0.0 0.0 copy-start.1
  0.0 2.3 %fusion.33 = (f32[6,64]{1,0:T(8,128)S(1)}, f32[6,64,512]{2,1,0:T(8,128)S(1)}) fusion(bf16[6,512,512]{2,1,0:T(8,128)(2,1)} %param.13, bf16[1,6,64,256]{3,1,2,0:T(8,128)(2,1)} %bitcast.32, s32[6]{0:T(128)} %param.15), kind=kOutput, calls=%fused_computation.33 | convolution fusion | flops 101449344 | bytes 2623488 | tf_op jit(solution)/shard_map/rhd,rld->rhl/dot_general | solution.py:27
  2.3 0.7 slice_convert_fusion
  3.0 1.1 %fusion.21 = f32[6,1,64]{2,1,0:T(1,128)S(1)} fusion(bf16[1,6,64,256]{3,1,2,0:T(8,128)(2,1)} %bitcast.33, bf16[6,256,1]{1,0,2:T(8,128)(2,1)S(1)} %get-tuple-element.8), kind=kOutput, calls=%fused_computation.17 | convolution fusion | flops 196608 | bytes 201216 | tf_op jit(solution)/shard_map/rhd,rd->rh/dot_general | solution.py:31
  4.1 0.0 copy-done.1
  4.1 0.3 fusion.16
  4.4 0.0 copy-done.2
  4.4 0.0 copy-start
  4.5 0.4 fusion.13
  4.9 0.1 convert_element_type.28
  5.0 0.1 copy.47
  5.2 0.7 pad.4.att
  5.9 0.0 copy-done
  5.9 0.6 reshape.14.gain
  6.5 98.3 %layer.1 = bf16[24,1792]{1,0:T(8,128)(2,1)} custom-call(bf16[4,8,4096]{2,1,0:T(8,128)(2,1)} %pad.4.att, bf16[24,1792]{1,0:T(8,128)(2,1)} %resid.1, f32[1,1792]{1,0:T(1,128)} %reshape.14.gain, bf16[24,32]{1,0:T(8,128)(2,1)} %constant.14.clone.pick_local, bf16[96,96]{1,0:T(8,128)(2,1)} %constant.15.clone.pick_all, bf16[4096,1792]{1,0:T(8,128)(2,1)} %wo_hbm.1, ...), custom_call_target="tpu_custom_call" | custom-call | tf_op jit(solution)/shard_map/layer/pallas_call | solution.py:540
  104.8 1.5 %copy.49 = bf16[24,1792]{1,0:T(8,128)(2,1)} copy(bf16[24,1792]{1,0:T(8,128)(2,1)} %layer.1) | data formatting | bytes 172032
  (2 shorter events, 0.0 us)
Async XLA Ops:
  0.0 4.4 %copy-start.2 = (bf16[6,512,512]{2,1,0:T(8,128)(2,1)S(1)}, bf16[6,512,512]{2,1,0:T(8,128)(2,1)}, u32[]{:S(2)}) copy-start(bf16[6,512,512]{2,1,0:T(8,128)(2,1)} %param.13) | copy-start | bytes 9437188
  0.0 4.1 %copy-start.1 = (s32[6]{0:T(128)S(1)}, s32[6]{0:T(128)}, u32[]{:S(2)}) copy-start(s32[6]{0:T(128)} %param.15) | copy-start | bytes 76
  4.4 1.5 %copy-start = (bf16[1792]{0:T(1024)(128)(2,1)S(1)}, bf16[1792]{0:T(1024)(128)(2,1)}, u32[]{:S(2)}) copy-start(bf16[1792]{0:T(1024)(128)(2,1)} %param.18) | copy-start | bytes 10756
